TPU v7x, 512 devices: a whole 4x8x8 slice. The times are simulated.
512 devices in a mesh: grp: 32 (over y_lo, z, core), blk: 16 (over x, y_hi).
Axes of the slice: x: 4, y: 8 (y_hi: 4, y_lo: 2; y = y_hi * 2 + y_lo), z: 8, core: 2. Of those that a mesh axis runs over, the one named last changes fastest.
Arguments:
- child_inverse: bfloat16 [32, 2, 2048, 2048], P('grp', None, 'blk'), may hold values from -0.09375 to 0.09375
- border_block: bfloat16 [32, 2, 2048, 2048], P('grp', None, 'blk'), may hold values from -0.09375 to 0.09375
- child_rhs: bfloat16 [32, 2, 2048, 256], P('grp', None, 'blk'), may hold values from -6 to 6
- parent_inverse: bfloat16 [32, 2, 4096, 2048], P('grp', None, 'blk'), may hold values from -0.0625 to 0.0625
- parent_rhs: bfloat16 [32, 2, 2048, 256], P('grp', None, 'blk'), may hold values from -6 to 6
- parent_of: int32 [32, 1], replicated, may hold values from 0 to 15
- owner: int32 [16], replicated, may hold values from 0 to 15, each once
- row_map: int32 [32, 2048], replicated, may hold values from 0 to 4095, as said below
Outputs:
- child_solution: bfloat16 [32, 2, 2048, 256], P('grp', None, 'blk')
- parent_solution: bfloat16 [32, 2, 2048, 256], P('grp', None, 'blk')
Inputs may be any that keep to these rules, and one draw needn't show every extreme that they name: parent_of[c, 0] is the parent front of the sibling front on group c; every parent front has one sibling or more. owner[p] names the pair of groups 2 owner[p] and 2 owner[p] + 1 that holds parent front p; each pair holds one parent. row_map[c, j] differ for different j of one c; border row j with j // 128 = b goes to a parent row h * 2048 + b * 128 + r with h of 0 or 1 and r < 128.
All inputs are finite; a program needn't handle non-finite values.
Results may differ from a plain program's by a relative error of at most 0.008.
Values may be sent and summed in bfloat16 or wider, within the bound.
No kernel may reach another device: no remote copies, remote signals or barrier semaphores. Data moves between devices by JAX's collectives and lax.ppermute only.
A program may use at most 64 MiB of HBM per device.

v0:
```python
import jax
import jax.numpy as jnp
from jax import lax
from jax.sharding import PartitionSpec as P


def swapped(shard, axis, stride):
    return lax.ppermute(shard, axis, [(i, i ^ 1 << stride) for i in range(lax.axis_size(axis))])


def complex_product(left, right):
    real_part = jnp.dot(left[0], right[0], preferred_element_type=jnp.float32) - jnp.dot(
        left[1], right[1], preferred_element_type=jnp.float32
    )
    imag_part = jnp.dot(left[0], right[1], preferred_element_type=jnp.float32) + jnp.dot(
        left[1], right[0], preferred_element_type=jnp.float32
    )
    return jnp.stack([real_part, imag_part])


def column_fold(matrix, shard_piece):
    return complex_product(matrix, shard_piece)


def per_device(
    child_inverse, border_block, child_rhs, parent_inverse, parent_rhs, parent_of, owner, row_map
):
    inverse_rows = child_inverse[0]
    border_rows_block = border_block[0]
    child_solved = column_fold(
        inverse_rows, lax.all_gather(child_rhs[0], "blk", axis=1, tiled=True)
    ).astype(jnp.bfloat16)
    update_rows = (
        -column_fold(border_rows_block, lax.all_gather(child_solved, "blk", axis=1, tiled=True))
    ).astype(jnp.bfloat16)
    group_index = lax.axis_index("grp")
    slot_index = lax.axis_index("blk")
    column_half = group_index % 2
    my_pair = group_index // 2
    border_count = update_rows.shape[1]
    half_rows = parent_rhs.shape[2]
    half_order = parent_inverse.shape[3]
    destination = owner[parent_of[:, 0]]
    local_map = lax.dynamic_slice_in_dim(row_map, slot_index * border_count, border_count, 1)
    row_base = slot_index * half_rows
    offsets = jnp.arange(half_rows, dtype=jnp.int32)
    wanted_rows = column_half * half_order + row_base + offsets
    matches = (local_map[:, None, :] == wanted_rows[None, :, None]) & (destination == my_pair)[
        :, None, None
    ]
    onehot_table = matches.astype(jnp.bfloat16)
    received_sums = jnp.einsum(
        "krj,kcjs->crs",
        onehot_table,
        lax.all_gather(update_rows[None], "grp", axis=0, tiled=True),
        preferred_element_type=jnp.float32,
    )
    right_side = (parent_rhs[0].astype(jnp.float32) + received_sums).astype(jnp.bfloat16)
    parent_block = parent_inverse[0]
    partial_value = column_fold(parent_block, lax.all_gather(right_side, "blk", axis=1, tiled=True))
    partner_part = swapped(partial_value.astype(jnp.bfloat16), "grp", 0).astype(partial_value.dtype)
    combined = partial_value + partner_part
    own_rows = lax.dynamic_slice_in_dim(combined, column_half * half_rows, half_rows, 1)
    return (child_solved[None], own_rows.astype(jnp.bfloat16)[None])


def solution(mesh):
    in_specs = (
        P("grp", None, "blk", None),
        P("grp", None, "blk", None),
        P("grp", None, "blk", None),
        P("grp", None, "blk", None),
        P("grp", None, "blk", None),
        P(),
        P(),
        P(),
    )
    out_specs = (P("grp", None, "blk", None), P("grp", None, "blk", None))
    return jax.shard_map(
        per_device, mesh=mesh, in_specs=in_specs, out_specs=out_specs, check_vma=False
    )
```

profile of v0, /device:TPU:1, one launch (start us, length us, event | category | flops | bytes accessed | tf_op | source)
XLA Modules:
  0.0 306.5 jit_solution(10172488542410082918)
XLA Ops:
  7.2 0.0 all-gather.12.cloned.1.call-start
  7.2 0.7 all-gather.12.cloned.1.call-update
  7.9 0.0 all-gather.6.cloned.1.call-start
  8.0 72.5 %all-gather.12.cloned.1.call-done = bf16[1,2,2048,256]{3,2,1,0:T(8,128)(2,1)} async-done(((bf16[1,2,128,256]{3,2,1,0:T(8,128)(2,1)}), bf16[1,2,2048,256]{3,2,1,0:T(8,128)(2,1)}) %all-gather.12.cloned.1.call-update) | async-done | bytes 2097168 | tf_op jit(solution)/shard_map/all_gather | solution.py:31
  80.5 1.8 fusion.28
  82.3 1.5 fusion.29
  83.9 0.3 fusion.17
  84.2 0.3 fusion.18
  84.5 0.7 pad_maximum_fusion.2
  85.2 0.0 all-gather.8.cloned.1.call-start
  85.3 62.4 %all-gather.6.cloned.1.call-done = bf16[2,2048,256]{2,1,0:T(8,128)(2,1)} async-done(((bf16[2,128,256]{2,1,0:T(8,128)(2,1)}), bf16[2,2048,256]{2,1,0:T(8,128)(2,1)}) %all-gather.6.cloned.1.call-update) | async-done | bytes 2097168 | tf_op jit(solution)/shard_map/all_gather | solution.py:34
  147.6 1.8 fusion.30
  149.5 0.1 copy-done.4
  149.5 0.5 fusion.31
  150.0 0.5 fusion.16
  150.5 0.5 fusion.15
  151.0 0.8 copy.17
  151.8 0.0 all-gather.10.cloned.1.call-start
  151.9 0.1 copy.16
  152.1 0.7 gather_fusion
  152.8 67.6 %all-gather.8.cloned.1.call-done = bf16[32,2,128,256]{3,2,1,0:T(8,128)(2,1)} async-done(((bf16[1,2,128,256]{3,2,1,0:T(8,128)(2,1)}), bf16[32,2,128,256]{3,2,1,0:T(8,128)(2,1)}) %all-gather.8.cloned.1.call-update) | async-done | bytes 4194320 | tf_op jit(solution)/shard_map/all_gather | solution.py:55
  220.4 4.3 %fusion.12 = bf16[2,128,256]{1,2,0:T(8,128)(2,1)} fusion(bf16[32,2,128,256]{3,2,1,0:T(8,128)(2,1)} %all-gather.8.cloned.1.call-done, s32[32,128]{1,0:T(8,128)S(1)} %constant_dynamic-slice_fusion, s32[128]{0:T(128)S(1)} %iota_add_fusion, pred[32]{0:T(512)(128)(4,1)S(1)} %broadcast_compare_fusion, bf16[1,2,128,256]{2,3,1,0:T(8,128)(2,1)S(1)} %copy.16), kind=kOutput, calls=%fused_computation.11 | convolution fusion | flops 538116096 | bytes 4473376 | tf_op jit(solution)/shard_map/krj,kcjs->crs/dot_general | solution.py:52
  224.7 64.1 %all-gather.10.cloned.1.call-done = bf16[2,2048,256]{1,2,0:T(8,128)(2,1)} async-done(((bf16[2,128,256]{1,2,0:T(8,128)(2,1)}), bf16[2,2048,256]{1,2,0:T(8,128)(2,1)}) %all-gather.10.cloned.1.call-update) | async-done | bytes 2097168 | tf_op jit(solution)/shard_map/all_gather | solution.py:60
  288.8 1.8 fusion.23
  290.7 0.1 copy-done.6
  290.7 0.5 fusion.21
  291.2 0.5 fusion.8
  291.7 0.5 fusion.7
  292.2 5.8 %collective-permute-start = (bf16[2,256,256]{1,2,0:T(8,128)(2,1)S(1)}, bf16[2,256,256]{1,2,0:T(8,128)(2,1)S(1)}, u32[]{:S(2)}, u32[]{:S(2)}) collective-permute-start(bf16[2,256,256]{1,2,0:T(8,128)(2,1)S(1)} %fusion.36), channel_id=1, source_target_pairs={{0,16},{16,0},{32,48},{48,32},{64,80},{80,64},{96,112},{112,96},{1... | collective-permute-start | bytes 786440 | tf_op jit(solution)/shard_map/ppermute | solution.py:8
  298.0 0.7 pad_maximum_fusion.1
  298.7 0.5 collective-permute-done
  299.2 0.8 copy.19
  (29 shorter events, 0.2 us)
Async XLA Ops:
  7.2 145.6 %copy-start = (s32[32,2048]{1,0:T(8,128)S(1)}, s32[32,2048]{1,0:T(8,128)}, u32[]{:S(2)}) copy-start(s32[32,2048]{1,0:T(8,128)} %param.15) | copy-start | bytes 786436
  7.2 75.1 %copy-start.7 = (bf16[1,2,128,2048]{3,2,1,0:T(8,128)(2,1)S(1)}, bf16[1,2,128,2048]{3,2,1,0:T(8,128)(2,1)}, u32[]{:S(2)}) copy-start(bf16[1,2,128,2048]{3,2,1,0:T(8,128)(2,1)} %param.8) | copy-start | bytes 3145732
  7.2 73.3 %all-gather.12.cloned.1.call-start = ((), (), s32[]{:S(2)}) async-start(), calls=%async_computation.3 | async-start | bytes 2228224 | tf_op jit(solution)/shard_map/all_gather | solution.py:31
  7.9 139.7 %all-gather.6.cloned.1.call-start = ((), (), s32[]{:S(2)}) async-start(), calls=%async_computation | async-start | bytes 2228224 | tf_op jit(solution)/shard_map/all_gather | solution.py:34
  80.5 3.4 %copy-start.5 = (bf16[1,2,2048,256]{3,2,1,0:T(8,128)(2,1)S(1)}, bf16[1,2,2048,256]{3,2,1,0:T(8,128)(2,1)}, u32[]{:S(2)}) copy-start(bf16[1,2,2048,256]{3,2,1,0:T(8,128)(2,1)} %all-gather.12.cloned.1.call-done) | copy-start | bytes 6291460
  83.9 63.8 %copy-start.8 = (bf16[1,2,128,2048]{3,2,1,0:T(8,128)(2,1)S(1)}, bf16[1,2,128,2048]{3,2,1,0:T(8,128)(2,1)}, u32[]{:S(2)}) copy-start(bf16[1,2,128,2048]{3,2,1,0:T(8,128)(2,1)} %param.9) | copy-start | bytes 3145732
  85.2 135.2 %all-gather.8.cloned.1.call-start = ((), (), s32[]{:S(2)}) async-start(), calls=%async_computation.1 | async-start | bytes 4325376 | tf_op jit(solution)/shard_map/all_gather | solution.py:55
  147.6 1.9 copy-start.4
  150.5 1.4 copy-start.2
  150.5 1.6 copy-start.9
  150.5 1.6 copy-start.1
  151.8 137.0 %all-gather.10.cloned.1.call-start = ((), (), s32[]{:S(2)}) async-start(), calls=%async_computation.2 | async-start | bytes 2228224 | tf_op jit(solution)/shard_map/all_gather | solution.py:60
  152.8 136.0 %copy-start.3 = (bf16[1,2,256,2048]{3,2,1,0:T(8,128)(2,1)S(1)}, bf16[1,2,256,2048]{3,2,1,0:T(8,128)(2,1)}, u32[]{:S(2)}) copy-start(bf16[1,2,256,2048]{3,2,1,0:T(8,128)(2,1)} %param.11) | copy-start | bytes 6291460
  288.8 1.9 copy-start.6
  292.2 6.9 %collective-permute-start = (bf16[2,256,256]{1,2,0:T(8,128)(2,1)S(1)}, bf16[2,256,256]{1,2,0:T(8,128)(2,1)S(1)}, u32[]{:S(2)}, u32[]{:S(2)}) collective-permute-start(bf16[2,256,256]{1,2,0:T(8,128)(2,1)S(1)} %fusion.36), channel_id=1, source_target_pairs={{0,16},{16,0},{32,48},{48,32},{64,80},{80,64},{96,112},{112,96},{1... | collective-permute-start | bytes 786440 | tf_op jit(solution)/shard_map/ppermute | solution.py:8
Sparse Core Ops, SparseCore 0:
  11.1 69.3 all-gather.11
  85.3 62.2 all-gather.5
  151.9 68.4 all-gather.7
  224.8 63.9 all-gather.9
where the time goes:
time: 307 us; the launch traced here: 306 us
  waiting for transfers between devices  268 us (87%)
  matrix products  14.8 us (5%)
  between operations  14.1 us (5%)
  starting transfers between devices  5.96 us (2%)
    all_gather x1, waiting for transfers between devices, per_device(): lax.all_gather(child_rhs[0], 'blk', axis=1, tiled=True)  72.5 us
    all_gather x1, waiting for transfers between devices, per_device(): lax.all_gather(update_rows[None], 'grp', axis=0, tiled=True)  67.6 us
    all_gather x1, waiting for transfers between devices, per_device(): lax.all_gather(right_side, 'blk', axis=1, tiled=True)  64.1 us
    all_gather x1, waiting for transfers between devices, per_device(): lax.all_gather(child_solved, 'blk', axis=1, tiled=True)  62.4 us
  transfers between devices with their start and end apart: 5, of which 5 were waited for; matrix products, arithmetic and copies ran while one was open for 0% of the time, Pallas kernels for 0%

commit v1 on v0

v1 whole, which is shorter than its diff:
```python
import functools

import jax
import jax.numpy as jnp
from jax import lax
from jax.experimental import pallas as pl
from jax.experimental.pallas import tpu as pltpu
from jax.sharding import PartitionSpec as P

F32 = jnp.float32
BF16 = jnp.bfloat16
GROUPS = 32
SIDE = 4
CHUNKS = 1
VM = pl.BlockSpec(memory_space=pltpu.VMEM)
SM = pl.BlockSpec(memory_space=pltpu.SMEM)


def cost(flops, moved):
    return pl.CostEstimate(flops=flops, bytes_accessed=moved, transcendentals=0)


def products(m_ref, g_ref):
    rows, inner = m_ref.shape[1:]
    cols = g_ref.shape[-1]
    both = m_ref[...].reshape(2 * rows, inner)
    with_real = jnp.dot(both, g_ref[:, 0].reshape(inner, cols), preferred_element_type=F32)
    with_imag = jnp.dot(both, g_ref[:, 1].reshape(inner, cols), preferred_element_type=F32)
    return with_real[:rows] - with_imag[rows:], with_imag[:rows] + with_real[rows:]


def solve_kernel(m_ref, g_ref, o_ref):
    real, imag = products(m_ref, g_ref)
    o_ref[0] = real.astype(BF16)
    o_ref[1] = imag.astype(BF16)


def update_kernel(m_ref, g_ref, o_ref):
    parts = products(m_ref, g_ref)
    wide = jnp.concatenate([-part.T for part in parts], axis=0)
    o_ref[...] = wide.astype(BF16).reshape(o_ref.shape)


def partial_kernel(half_ref, m_ref, g_ref, kept_ref, given_ref, full_ref):
    rows = kept_ref.shape[1]
    for part, value in enumerate(products(m_ref, g_ref)):
        full_ref[part] = value
    half = half_ref[0]
    mine = pl.ds(pl.multiple_of(half * rows, rows), rows)
    other = pl.ds(pl.multiple_of((1 - half) * rows, rows), rows)
    kept_ref[...] = full_ref[:, mine, :]
    given_ref[...] = full_ref[:, other, :].astype(BF16)


def route_kernel(parent_ref, owner_ref, rows_ref, v_ref, o_ref, sums_ref):
    rows = v_ref.shape[2]
    sums_ref[...] = jnp.zeros_like(sums_ref)
    slots = lax.broadcasted_iota(jnp.int32, (2 * rows, rows), 0)
    for child in range(GROUPS):
        wanted = jnp.broadcast_to(rows_ref[child : child + 1, :], (2 * rows, rows))
        table = jnp.where(slots == wanted, 1.0, 0.0).astype(BF16)
        placed = lax.dot_general(
            v_ref[child], table, (((1,), (1,)), ((), ())), preferred_element_type=F32
        )
        pair = owner_ref[parent_ref[child]]
        sums_ref[pair] += placed
    for pair in range(GROUPS // 2):
        for half in range(2):
            o_ref[2 * pair + half] = sums_ref[pair, :, half * rows : (half + 1) * rows].astype(BF16)


def right_kernel(b_ref, p_ref, o_ref):
    cols = p_ref.shape[2]
    flat = b_ref[...].reshape(2 * cols, b_ref.shape[2]).astype(F32)
    for part in range(2):
        o_ref[part] = (
            p_ref[part].astype(F32) + flat[part * cols : (part + 1) * cols].T
        ).astype(BF16)


def solve(matrix, gathered):
    rows, inner = matrix.shape[1:]
    cols = gathered.shape[-1]
    return pl.pallas_call(
        solve_kernel,
        out_shape=jax.ShapeDtypeStruct((2, rows, cols), BF16),
        in_specs=[VM, VM],
        out_specs=VM,
        cost_estimate=cost(8 * rows * inner * cols, 4 * inner * (rows + cols)),
    )(matrix, gathered)


def updates(matrix, gathered):
    rows, inner = matrix.shape[1:]
    cols = gathered.shape[-1]
    return pl.pallas_call(
        update_kernel,
        out_shape=jax.ShapeDtypeStruct((GROUPS, 2 * cols // GROUPS, rows), BF16),
        in_specs=[VM, VM],
        out_specs=VM,
        cost_estimate=cost(8 * rows * inner * cols, 4 * inner * (rows + cols)),
    )(matrix, gathered)


def partial(half, matrix, gathered):
    rows, inner = matrix.shape[1:]
    cols = gathered.shape[-1]
    return pl.pallas_call(
        partial_kernel,
        out_shape=(
            jax.ShapeDtypeStruct((2, rows // 2, cols), F32),
            jax.ShapeDtypeStruct((2, rows // 2, cols), BF16),
        ),
        in_specs=[SM, VM, VM],
        out_specs=(VM, VM),
        scratch_shapes=[pltpu.VMEM((2, rows, cols), F32)],
        cost_estimate=cost(8 * rows * inner * cols, 4 * inner * (rows + cols)),
    )(half, matrix, gathered)


def route(parent_of, owner, rows_of, pieces):
    width, rows = pieces.shape[1:]
    return pl.pallas_call(
        route_kernel,
        out_shape=jax.ShapeDtypeStruct(pieces.shape, BF16),
        in_specs=[SM, SM, VM, VM],
        out_specs=VM,
        scratch_shapes=[pltpu.VMEM((GROUPS // 2, width, 2 * rows), F32)],
        cost_estimate=cost(4 * GROUPS * width * rows * rows, 4 * GROUPS * width * rows),
    )(parent_of, owner, rows_of, pieces)


def right_side(back, parent_rhs):
    return pl.pallas_call(
        right_kernel,
        out_shape=jax.ShapeDtypeStruct(parent_rhs.shape, BF16),
        in_specs=[VM, VM],
        out_specs=VM,
        cost_estimate=cost(2 * parent_rhs.size, 6 * parent_rhs.size),
    )(back, parent_rhs)


def fanned(block, groups):
    copies = jnp.broadcast_to(block[None], (len(groups[0]),) + block.shape)
    return lax.all_to_all(copies, "blk", 0, 0, axis_index_groups=groups, tiled=True)


def gathered(block):
    along_y = [[i * SIDE + j for j in range(SIDE)] for i in range(SIDE)]
    along_x = [[i * SIDE + j for i in range(SIDE)] for j in range(SIDE)]
    whole = fanned(fanned(block, along_y), along_x)
    return whole.reshape((SIDE * SIDE,) + block.shape)


def exchanged(pieces):
    return lax.all_to_all(pieces, "grp", 0, 0, tiled=True)


def per_device(
    child_inverse, border_block, child_rhs, parent_inverse, parent_rhs, parent_of, owner, row_map
):
    slot_index = lax.axis_index("blk")
    half = jnp.reshape(lax.axis_index("grp") % 2, (1,)).astype(jnp.int32)
    rows, cols = child_rhs.shape[2:]
    local_map = lax.dynamic_slice_in_dim(row_map, slot_index * rows, rows, 1)
    half_order = 16 * rows
    rows_of = (local_map // half_order) * rows + local_map % rows
    parents = parent_of[:, 0]
    width = cols // CHUNKS

    solutions, answers = [], []
    for chunk in range(CHUNKS):
        here = slice(chunk * width, (chunk + 1) * width)
        solved = solve(child_inverse[0], gathered(child_rhs[0][:, :, here]))
        pieces = updates(border_block[0], gathered(solved))
        sums = exchanged(route(parents, owner, rows_of, exchanged(pieces)))
        right = right_side(sums, parent_rhs[0][:, :, here])
        kept, given = partial(half, parent_inverse[0], gathered(right))
        taken = lax.ppermute(given, "grp", [(i, i ^ 1) for i in range(GROUPS)])
        solutions.append(solved)
        answers.append((kept + taken.astype(F32)).astype(BF16))
    if CHUNKS == 1:
        return solutions[0][None], answers[0][None]
    return jnp.concatenate(solutions, -1)[None], jnp.concatenate(answers, -1)[None]


def solution(mesh):
    spec = P("grp", None, "blk", None)
    return jax.shard_map(
        per_device,
        mesh=mesh,
        in_specs=(spec,) * 5 + (P(), P(), P()),
        out_specs=(spec, spec),
        check_vma=False,
    )
```

time: 307 us -> 208 us (0.68)
  waiting for transfers between devices: 268 us -> 31.2 us
  blocking collectives: 0 us -> 124 us
  starting transfers between devices: 5.96 us -> 25.4 us
  Pallas kernels: 0 us -> 14.9 us
  matrix products: 14.8 us -> 0 us
  between operations: 14.1 us -> 0.7 us
  local copies, waits for them, and re-layouts: 2.54 us -> 6.9 us
    all_gather x4 -> x0, waiting for transfers between devices: 266 us -> none  [the longest x1 72.5 us: per_device(): lax.all_gather(child_rhs[0], 'blk', axis=1, tiled=True)]
    all_to_all x0 -> x6, blocking collectives: none -> 124 us  [the longest x5 111 us: fanned(): lax.all_to_all(copies, 'blk', 0, 0, axis_index_groups=groups, tiled=True)]
    all_to_all x0 -> x2, waiting for transfers between devices: none -> 30 us  [the longest x1 22.5 us: fanned(): lax.all_to_all(copies, 'blk', 0, 0, axis_index_groups=groups, tiled=True)]
    all_to_all x0 -> x2, starting transfers between devices: none -> 18.8 us  [the longest x1 15.2 us: exchanged(): return lax.all_to_all(pieces, 'grp', 0, 0, tiled=True)]
    pallas_call x0 -> x5, Pallas kernels: none -> 14.9 us  [the longest x1 4.23 us: partial(): pl.pallas_call(partial_kernel, out_shape=(jax.ShapeDtypeStruct((2, rows /...]
    dot_general x13 -> x0, matrix products: 14.8 us -> none  [the longest x3 5.52 us: complex_product(): jnp.dot(left[0], right[0], preferred_element_type=jnp.float32)]
    broadcast_in_dim x0 -> x6, local copies, waits for them, and re-layouts: none -> 4.9 us  [fanned(): copies = jnp.broadcast_to(block[None], (len(groups[0]),) + block.shape)]
  transfers between devices with their start and end apart: 5 -> 3, of which waited for: 5 -> 3; matrix products, arithmetic and copies ran while one was open for 0% -> 1% of each run, Pallas kernels for 0% -> 0%
where the time goes in v1:
time: 208 us; the launch traced here: 207 us
  blocking collectives  124 us (60%)
  waiting for transfers between devices  31.2 us (15%)
  starting transfers between devices  25.4 us (12%)
  Pallas kernels  14.9 us (7%)
  local copies, waits for them, and re-layouts  6.9 us (3%)
  other arithmetic  2.97 us (1%)
    all_to_all x5, blocking collectives, fanned(): lax.all_to_all(copies, 'blk', 0, 0, axis_index_groups=groups, tiled=True)  111 us
    all_to_all x1, waiting for transfers between devices, fanned(): lax.all_to_all(copies, 'blk', 0, 0, axis_index_groups=groups, tiled=True)  22.5 us
    all_to_all x1, starting transfers between devices, exchanged(): return lax.all_to_all(pieces, 'grp', 0, 0, tiled=True)  15.2 us
    all_to_all x1, blocking collectives, exchanged(): return lax.all_to_all(pieces, 'grp', 0, 0, tiled=True)  13.6 us
    all_to_all x1, waiting for transfers between devices, exchanged(): return lax.all_to_all(pieces, 'grp', 0, 0, tiled=True)  7.52 us
    ppermute x1, starting transfers between devices, per_device(): taken = lax.ppermute(given, 'grp', [(i, i ^ 1) for i in range(GROUPS)])  6.63 us
    broadcast_in_dim x6, local copies, waits for them, and re-layouts, fanned(): copies = jnp.broadcast_to(block[None], (len(groups[0]),) + block.shape)  4.9 us
    pallas_call x1, Pallas kernels, partial(): pl.pallas_call(partial_kernel, out_shape=(jax.ShapeDtypeStruct((2, rows /...  4.23 us
  transfers between devices with their start and end apart: 3, of which 3 were waited for; matrix products, arithmetic and copies ran while one was open for 1% of the time, Pallas kernels for 0%

profile of v1, /device:TPU:1, one launch (start us, length us, event | category | flops | bytes accessed | tf_op | source)
XLA Modules:
  0.0 206.5 jit_solution(6039156566181932877)
XLA Ops:
  0.6 0.9 broadcast_in_dim.19
  1.6 21.9 %all_to_all.40 = bf16[4,2,128,256]{3,2,1,0:T(8,128)(2,1)S(1)} all-to-all(bf16[4,2,128,256]{3,2,1,0:T(8,128)(2,1)S(1)} %broadcast_in_dim.19), channel_id=1, replica_groups={{0,1,2,3},{4,5,6,7},{8,9,10,11},{12,13,14,15},{16,17,18,19},{20,21,22,2..., dimensions={0} | all-to-all | bytes 1048576 | tf_op jit(solution)/shard_map/all_to_all | solution.py:145
  23.5 0.2 broadcast_in_dim.20
  23.7 28.7 %all_to_all.41 = bf16[4,4,2,128,256]{4,3,2,1,0:T(8,128)(2,1)} all-to-all(bf16[4,4,2,128,256]{4,3,2,1,0:T(8,128)(2,1)S(1)} %broadcast_in_dim.20), channel_id=1, replica_groups={{0,4,8,12},{1,5,9,13},{2,6,10,14},{3,7,11,15},{16,20,24,28},{17,21,25,2..., dimensions={0} | all-to-all | bytes 4194304 | tf_op jit(solution)/shard_map/all_to_all | solution.py:145
  52.4 3.3 %shard_map.95 = bf16[2,128,256]{2,1,0:T(8,128)(2,1)} custom-call(bf16[2,128,2048]{2,1,0:T(8,128)(2,1)} %bitcast.17, bf16[16,2,128,256]{3,2,1,0:T(8,128)(2,1)} %bitcast.14), custom_call_target="tpu_custom_call" | custom-call | flops 536870912 | bytes 3145728 | tf_op jit(solution)/shard_map/pallas_call | solution.py:84
  55.7 0.9 broadcast_in_dim.22
  56.7 16.9 %all_to_all.42 = bf16[4,2,128,256]{3,2,1,0:T(8,128)(2,1)S(1)} all-to-all(bf16[4,2,128,256]{3,2,1,0:T(8,128)(2,1)S(1)} %broadcast_in_dim.22), channel_id=1, replica_groups={{0,1,2,3},{4,5,6,7},{8,9,10,11},{12,13,14,15},{16,17,18,19},{20,21,22,2..., dimensions={0} | all-to-all | bytes 1048576 | tf_op jit(solution)/shard_map/all_to_all | solution.py:145
  73.6 0.2 broadcast_in_dim.23
  73.9 25.8 %all_to_all.43 = bf16[4,4,2,128,256]{4,3,2,1,0:T(8,128)(2,1)} all-to-all(bf16[4,4,2,128,256]{4,3,2,1,0:T(8,128)(2,1)S(1)} %broadcast_in_dim.23), channel_id=1, replica_groups={{0,4,8,12},{1,5,9,13},{2,6,10,14},{3,7,11,15},{16,20,24,28},{17,21,25,2..., dimensions={0} | all-to-all | bytes 4194304 | tf_op jit(solution)/shard_map/all_to_all | solution.py:145
  99.7 3.4 %shard_map.96 = bf16[32,16,128]{2,1,0:T(8,128)(2,1)} custom-call(bf16[2,128,2048]{2,1,0:T(8,128)(2,1)} %bitcast.18, bf16[16,2,128,256]{3,2,1,0:T(8,128)(2,1)} %bitcast.15), custom_call_target="tpu_custom_call" | custom-call | flops 536870912 | bytes 3145728 | tf_op jit(solution)/shard_map/pallas_call | solution.py:96
  103.1 15.2 %all-to-all-start.4 = ((bf16[32,16,128]{2,1,0:T(8,128)(2,1)}), bf16[32,16,128]{2,1,0:T(8,128)(2,1)S(1)}, u32[]{:S(2)}, u32[]{:S(2)}) async-start(bf16[32,16,128]{2,1,0:T(8,128)(2,1)} %shard_map.96), calls=%async_computation.4 | async-start | bytes 262144 | tf_op jit(solution)/shard_map/all_to_all | solution.py:156
  118.3 1.3 fusion.3.rows_ref
  119.6 7.5 %all-to-all-done.4.v_ref = bf16[32,16,128]{2,1,0:T(8,128)(2,1)S(1)} async-done(((bf16[32,16,128]{2,1,0:T(8,128)(2,1)}), bf16[32,16,128]{2,1,0:T(8,128)(2,1)S(1)}, u32[]{:S(2)}, u32[]{:S(2)}) %all-to-all-start.4) | async-done | bytes 131104 | tf_op jit(solution)/shard_map/all_to_all | solution.py:156
  127.1 0.0 copy-start.1
  127.1 0.7 copy-done.1
  127.8 2.3 %shard_map.97 = bf16[32,16,128]{2,1,0:T(8,128)(2,1)} custom-call(s32[32]{0:T(128)} %bitcast.22, s32[16]{0:T(128)} %owner_ref.1, s32[32,128]{1,0:T(8,128)} %fusion.3.rows_ref, bf16[32,16,128]{2,1,0:T(8,128)(2,1)} %copy-done.1), custom_call_target="tpu_custom_call" | custom-call | flops 33554432 | bytes 262144 | tf_op jit(solution)/shard_map/pallas_call | solution.py:123
  130.0 13.6 %all_to_all.44.b_ref = bf16[32,16,128]{2,1,0:T(8,128)(2,1)} all-to-all(bf16[32,16,128]{2,1,0:T(8,128)(2,1)} %shard_map.97), channel_id=1, replica_groups=mesh['grp'=32,'blk'=16] {'grp'}, dimensions={0} | all-to-all | bytes 262144 | tf_op jit(solution)/shard_map/all_to_all | solution.py:156
  143.7 1.7 shard_map.98
  145.4 0.9 broadcast_in_dim.24
  146.3 17.4 %all_to_all.45 = bf16[4,2,128,256]{3,2,1,0:T(8,128)(2,1)S(1)} all-to-all(bf16[4,2,128,256]{3,2,1,0:T(8,128)(2,1)S(1)} %broadcast_in_dim.24), channel_id=1, replica_groups={{0,1,2,3},{4,5,6,7},{8,9,10,11},{12,13,14,15},{16,17,18,19},{20,21,22,2..., dimensions={0} | all-to-all | bytes 1048576 | tf_op jit(solution)/shard_map/all_to_all | solution.py:145
  163.8 1.6 broadcast_in_dim.50
  165.4 3.6 %all-to-all-start.7 = ((bf16[4,4,2,128,256]{4,3,2,1,0:T(8,128)(2,1)}), bf16[4,4,2,128,256]{4,3,2,1,0:T(8,128)(2,1)S(1)}, u32[]{:S(2)}, u32[]{:S(2)}) async-start(bf16[4,4,2,128,256]{4,3,2,1,0:T(8,128)(2,1)} %broadcast_in_dim.50), calls=%async_computation.7 | async-start | bytes 4194304 | tf_op jit(solution)/shard_map/all_to_all | solution.py:145
  169.0 22.5 %all-to-all-done.7 = bf16[4,4,2,128,256]{4,3,2,1,0:T(8,128)(2,1)S(1)} async-done(((bf16[4,4,2,128,256]{4,3,2,1,0:T(8,128)(2,1)}), bf16[4,4,2,128,256]{4,3,2,1,0:T(8,128)(2,1)S(1)}, u32[]{:S(2)}, u32[]{:S(2)}) %all-to-all-start.7) | async-done | bytes 2097184 | tf_op jit(solution)/shard_map/all_to_all | solution.py:145
  191.5 0.0 copy-start
  191.5 1.3 copy-done
  192.8 4.2 %shard_map.99 = (f32[2,128,256]{2,1,0:T(8,128)}, bf16[2,128,256]{2,1,0:T(8,128)(2,1)}) custom-call(s32[1]{0:T(128)} %bitcast.4.half_ref, bf16[2,256,2048]{2,1,0:T(8,128)(2,1)} %bitcast.16, bf16[16,2,128,256]{3,2,1,0:T(8,128)(2,1)} %bitcast.13), custom_call_target="tpu_custom_call" | custom-call | flops 1073741824 | bytes 4194304 | tf_op jit(solution)/shard_map/pallas_call | solution.py:108
  197.1 6.6 %collective-permute-start = (bf16[2,128,256]{2,1,0:T(8,128)(2,1)}, bf16[2,128,256]{2,1,0:T(8,128)(2,1)S(1)}, u32[]{:S(2)}, u32[]{:S(2)}) collective-permute-start(bf16[2,128,256]{2,1,0:T(8,128)(2,1)} %get-tuple-element.5), channel_id=1, source_target_pairs={{0,16},{16,0},{32,48},{48,32},{64,80},{80,64},{96,112},{112,96},{1... | collective-permute-start | bytes 393224 | tf_op jit(solution)/shard_map/ppermute | solution.py:179
  203.7 1.2 collective-permute-done
  204.9 1.6 fusion
Async XLA Ops:
  103.1 24.1 %all-to-all-start.4 = ((bf16[32,16,128]{2,1,0:T(8,128)(2,1)}), bf16[32,16,128]{2,1,0:T(8,128)(2,1)S(1)}, u32[]{:S(2)}, u32[]{:S(2)}) async-start(bf16[32,16,128]{2,1,0:T(8,128)(2,1)} %shard_map.96), calls=%async_computation.4 | async-start | bytes 262144 | tf_op jit(solution)/shard_map/all_to_all | solution.py:156
  127.1 0.7 copy-start.1
  165.4 26.1 %all-to-all-start.7 = ((bf16[4,4,2,128,256]{4,3,2,1,0:T(8,128)(2,1)}), bf16[4,4,2,128,256]{4,3,2,1,0:T(8,128)(2,1)S(1)}, u32[]{:S(2)}, u32[]{:S(2)}) async-start(bf16[4,4,2,128,256]{4,3,2,1,0:T(8,128)(2,1)} %broadcast_in_dim.50), calls=%async_computation.7 | async-start | bytes 4194304 | tf_op jit(solution)/shard_map/all_to_all | solution.py:145
  191.5 1.3 copy-start
  197.1 7.8 %collective-permute-start = (bf16[2,128,256]{2,1,0:T(8,128)(2,1)}, bf16[2,128,256]{2,1,0:T(8,128)(2,1)S(1)}, u32[]{:S(2)}, u32[]{:S(2)}) collective-permute-start(bf16[2,128,256]{2,1,0:T(8,128)(2,1)} %get-tuple-element.5), channel_id=1, source_target_pairs={{0,16},{16,0},{32,48},{48,32},{64,80},{80,64},{96,112},{112,96},{1... | collective-permute-start | bytes 393224 | tf_op jit(solution)/shard_map/ppermute | solution.py:179
